TPU v7x, 32 devices: a whole 2x2x4 slice. The times are simulated.
32 devices in a mesh: section: 4 (over y, core), space: 8 (over z, x).
Axes of the slice: x: 2, y: 2, z: 4, core: 2. Of those that a mesh axis runs over, the one named last changes fastest.
Arguments:
- features: bfloat16 [4, 2048, 256], P('section', 'space'), may hold values from -6 to 6
- out_grad: bfloat16 [4, 2048, 256], P('section', 'space'), may hold values from -6 to 6
- weight: bfloat16 [4, 27, 256, 256], P('section'), may hold values from -0.078125 to 0.078125
- counts: int32 [4, 16], P('section', 'space'), may hold values from 16 to 128
- local_rows: int32 [4, 27, 2048], P('section', None, 'space'), may hold values from -1 to 255, as said below
- send_rows: int32 [4, 8, 27, 8, 2], P('section', 'space'), may hold values from -1 to 255, as said below
- recv_rows: int32 [4, 8, 27, 8, 2], P('section', 'space'), may hold values from -1 to 255, as said below
Outputs:
- handoff: bfloat16 [4, 2048, 256], P('section', 'space')
- weight_grad: float32 [4, 6912, 256], P('section', 'space')
Inputs may be any that keep to these rules, and one draw needn't show every extreme that they name: `local_rows`: -1 where a voxel has no pair on its own device at that offset. `send_rows`: for each offset and two different devices, the first 1 to 2 slots are used and the rest are -1; a device's slots to itself are all -1; for every sending device there is one offset at which all 2 slots to every other device are used. `recv_rows`: slot for slot the pairs of send_rows seen from the receiving device, -1 in the same empty slots.
All inputs are finite; a program needn't handle non-finite values.
Results may differ from a plain program's by a relative error of at most 0.0019.
Values may be sent and summed in bfloat16 or wider, within the bound.
No kernel may reach another device: no remote copies, remote signals or barrier semaphores. Data moves between devices by JAX's collectives and lax.ppermute only.
A program may use at most 64 MiB of HBM per device.

v0:
```python
import jax
import jax.numpy as jnp
from jax import lax
from jax.sharding import PartitionSpec as P

BLOCK = 128


def from_behind(block, axis, distance):
    devices = range(lax.axis_size(axis))
    route = [(i - distance, i) for i in devices if i - distance in devices]
    return lax.ppermute(block, axis, route)


def take_rows(source, row_index, nothing):
    picked = jnp.take(source, jnp.maximum(row_index, 0), axis=0)
    return jnp.where((row_index >= 0)[..., None], picked, nothing)


def body(features, out_grad, weight, counts, local_rows, send_rows, recv_rows):
    inputs = features[0]
    gradient = out_grad[0]
    kernel = weight[0]
    rows_dev = inputs.shape[0]
    channels = inputs.shape[1]
    offsets = kernel.shape[0]
    inside = (jnp.arange(BLOCK, dtype=jnp.int32)[None, :] < counts[0][:, None]).reshape(rows_dev, 1)
    nothing = jnp.zeros((), inputs.dtype)
    xmask = jnp.where(inside, inputs, nothing)
    gmask = jnp.where(inside, gradient, nothing)
    local_map = local_rows[0].T
    gathered = take_rows(gmask, local_map, nothing)
    input_grad = lax.dot_general(
        gathered, kernel, (((1, 2), (0, 1)), ((), ())), preferred_element_type=jnp.float32
    )
    weight_grad = lax.dot_general(
        gathered, xmask, (((0,), (0,)), ((), ())), preferred_element_type=jnp.float32
    )
    send_map = send_rows[0, 0]
    recv_map = recv_rows[0, 0]
    flat_shape = (offsets, -1, channels)
    outgoing = take_rows(gmask, send_map, nothing)
    partial_value = (
        lax.dot_general(
            outgoing.reshape(flat_shape),
            kernel,
            (((2,), (1,)), ((0,), (0,))),
            preferred_element_type=jnp.float32,
        )
        .astype(jnp.bfloat16)
        .reshape(outgoing.shape)
    )
    arrived = lax.all_to_all(partial_value, "space", split_axis=1, concat_axis=1, tiled=True)
    returned = lax.all_to_all(
        take_rows(xmask, recv_map, nothing), "space", split_axis=1, concat_axis=1, tiled=True
    )
    weight_grad = weight_grad + lax.dot_general(
        outgoing.reshape(flat_shape),
        returned.reshape(flat_shape),
        (((1,), (1,)), ((0,), (0,))),
        preferred_element_type=jnp.float32,
    )
    incoming = arrived.reshape(-1, channels).astype(jnp.float32)
    target = jnp.where(recv_map >= 0, recv_map, rows_dev).reshape(-1)
    input_grad = input_grad.at[target].add(incoming, mode="drop")
    result = jnp.where(inside, input_grad, 0.0).astype(jnp.bfloat16)
    handoff = from_behind(result, "section", -1)
    loss_scale = float(rows_dev * lax.axis_size("space")) ** (-0.5)
    summed = lax.psum_scatter(
        (weight_grad * loss_scale).reshape(offsets * channels, channels),
        "space",
        scatter_dimension=0,
        tiled=True,
    )
    return (handoff[None], summed[None])


def solution(mesh):
    placed = (
        P("section", "space", None),
        P("section", "space", None),
        P("section", None, None, None),
        P("section", "space"),
        P("section", None, "space"),
        P("section", "space", None, None, None),
        P("section", "space", None, None, None),
    )
    return jax.shard_map(
        body,
        mesh=mesh,
        in_specs=placed,
        out_specs=(P("section", "space", None), P("section", "space", None)),
        check_vma=False,
    )
```

profile of v0, /device:TPU:0, one launch (start us, length us, event | category | flops | bytes accessed | tf_op | source)
XLA Modules:
  0.0 275.7 jit_solution(11968080390307770625)
XLA Ops:
  7.2 0.0 copy-start
  7.2 0.9 compare_bitcast_fusion.1
  8.0 0.9 compare_and_fusion.1
  8.9 1.3 compare_bitcast_fusion.2
  10.2 0.8 copy.86
  11.0 0.8 copy.85
  11.8 0.8 copy.87
  12.5 1.0 reshape.142
  13.6 1.7 bitcast_select_fusion.1
  15.3 3.1 %gather_fusion.1 = bf16[432,256]{1,0:T(8,128)(2,1)} fusion(bf16[256,256]{1,0:T(8,128)(2,1)} %bitcast_select_fusion.1, s32[1024]{0:T(1024)S(1)} %pad_clamp_fusion.2), kind=kCustom, calls=%fused_computation.clone | custom fusion | bytes 444096 | tf_op jit(solution)/shard_map/jit(_take)/gather | solution.py:16
  18.4 1.7 reshape.145
  20.1 2.3 broadcast_select_fusion.3
  22.4 0.8 copy.89
  23.3 1.7 reshape.99
  25.0 0.0 copy-done
  25.0 2.2 fusion.4
  27.2 1.7 reshape.100
  28.9 1.8 copy.90
  30.7 7.3 %all-to-all-start = ((bf16[27,8,2,256]{3,2,0,1:T(2,128)(2,1)}), bf16[27,8,2,256]{3,2,0,1:T(2,128)(2,1)}, u32[]{:S(2)}, u32[]{:S(2)}) async-start(bf16[27,8,2,256]{3,2,0,1:T(2,128)(2,1)} %copy.90), calls=%async_computation | async-start | bytes 442368 | tf_op jit(solution)/shard_map/all_to_all | solution.py:53
  38.0 0.0 reduce-scatter.2.cloned.1.call-start
  38.0 0.0 copy-done.4
  38.0 0.6 compare_bitcast_fusion
  38.6 0.6 compare_and_fusion
  39.2 0.8 broadcast_maximum_fusion
  40.0 0.0 copy-start.3
  40.0 1.4 broadcast_compare_fusion
  41.4 0.0 copy-done.3
  41.4 1.5 copy.102
  42.9 0.8 copy.84
  43.7 0.7 copy.81
  44.4 1.5 copy.101
  45.9 1.4 copy.95
  47.3 1.4 copy.94
  48.8 1.7 reshape.122
  50.5 1.4 pad_clamp_fusion
  51.9 1.5 copy.96
  53.3 1.0 reshape.146
  54.4 1.0 squeeze.16
  55.4 18.5 %gather_fusion = bf16[6912,256]{1,0:T(8,128)(2,1)} fusion(bf16[256,256]{1,0:T(8,128)(2,1)} %bitcast_select_fusion.1, s32[7168]{0:T(1024)} %pad_clamp_fusion), kind=kCustom, calls=%fused_computation.2 | custom fusion | bytes 7105536 | tf_op jit(solution)/shard_map/jit(_take)/gather | solution.py:16
  73.9 6.4 %reshape.121 = bf16[256,27,256]{2,1,0:T(8,128)(2,1)} reshape(bf16[6912,256]{1,0:T(8,128)(2,1)} %gather_fusion) | data formatting | bytes 7077888 | tf_op jit(solution)/shard_map/jit(_take)/gather | solution.py:16
  80.3 7.6 %select_select_fusion = bf16[256,27,256]{2,1,0:T(8,128)(2,1)} fusion(bf16[256,27,256]{2,1,0:T(8,128)(2,1)} %reshape.121, pred[256,27]{1,0:T(8,128)(4,1)} %copy.81, pred[256,27]{1,0:T(8,128)(4,1)} %bitcast.53), kind=kLoop, calls=%fused_computation.5 | loop fusion | flops 3538944 | bytes 7091712 | tf_op jit(solution)/shard_map/jit(_where)/select_n | solution.py:17
  87.9 7.4 %copy.93 = bf16[256,27,256]{0,2,1:T(8,128)(2,1)} copy(bf16[256,27,256]{2,1,0:T(8,128)(2,1)} %select_select_fusion) | data formatting | bytes 7077888 | tf_op jit(solution)/shard_map/jit(_where)/select_n | solution.py:17
  95.3 3.8 %fusion.7 = f32[256,256]{1,0:T(8,128)} fusion(bf16[256,27,256]{0,2,1:T(8,128)(2,1)} %copy.93, bf16[1,27,256,256]{3,2,1,0:T(8,128)(2,1)S(1)} %copy-done), kind=kOutput, calls=%fused_computation.11 | convolution fusion | flops 905969664 | bytes 7340032 | tf_op jit(solution)/shard_map/dot_general | solution.py:33
  99.1 0.0 all-to-all-done
  99.1 1.0 copy_convert_fusion
  100.1 1.0 copy.92
  101.1 2.1 reshape.132
  103.1 4.7 %scatter_fusion = f32[256,256]{1,0:T(8,128)} fusion(f32[256,256]{1,0:T(8,128)} %fusion.7, s32[432]{0:T(512)S(1)} %bitcast.54, f32[432,256]{1,0:T(8,128)} %reshape.132), kind=kCustom, calls=%fused_computation.3 | custom fusion | flops 110592 | bytes 1328832 | tf_op jit(solution)/shard_map/scatter-add | solution.py:65
  107.9 0.0 copy-done.5
  107.9 1.8 bitcast_select_fusion
  109.7 3.1 %gather_fusion.2 = bf16[432,256]{1,0:T(8,128)(2,1)} fusion(bf16[256,256]{1,0:T(8,128)(2,1)} %get-tuple-element.7, s32[1024]{0:T(1024)S(1)} %pad_clamp_fusion.1), kind=kCustom, calls=%fused_computation.1.clone | custom fusion | bytes 444096 | tf_op jit(solution)/shard_map/jit(_take)/gather | solution.py:16
  112.8 1.7 reshape.149
  114.5 2.3 broadcast_select_fusion.2
  116.8 13.7 %all_to_all.10 = bf16[27,8,2,256]{3,2,0,1:T(2,128)(2,1)S(1)} all-to-all(bf16[27,8,2,256]{3,2,0,1:T(2,128)(2,1)S(1)} %broadcast_select_fusion.2), channel_id=1, replica_groups=mesh['section'=4,'space'=8] {'space'}, dimensions={1} | all-to-all | bytes 442368 | tf_op jit(solution)/shard_map/all_to_all | solution.py:54
  130.5 0.8 copy.98
  131.4 1.7 reshape.101
  133.1 2.3 fusion.11
  135.4 0.0 copy-done.1
  135.4 4.0 %add_multiply_fusion = f32[27,256,256]{2,1,0:T(8,128)} fusion(f32[27,256,256]{2,1,0:T(8,128)S(1)} %fusion.11, bf16[256,27,256]{0,2,1:T(8,128)(2,1)S(1)} %copy-done.1, bf16[256,256]{1,0:T(8,128)(2,1)S(1)} %copy-done.2), kind=kOutput, calls=%fused_computation.4 | convolution fusion | flops 909508608 | bytes 17825792 | tf_op jit(solution)/shard_map/dot_general | solution.py:36
  139.4 0.0 reduce-scatter.2.cloned.1.call-update
  139.4 1.3 collective-permute-start
  140.7 2.3 collective-permute-done
  143.0 124.3 %reduce-scatter.2.cloned.1.call-done = f32[864,256]{1,0:T(8,128)} async-done(((f32[6912,256]{1,0:T(8,128)}), f32[864,256]{1,0:T(8,128)}) %reduce-scatter.2.cloned.1.call-update) | async-done | bytes 884752 | tf_op jit(solution)/shard_map/reduce_scatter | solution.py:69
  267.3 1.6 copy.109
  (9 shorter events, 0.0 us)
Async XLA Ops:
  7.2 17.8 %copy-start = (bf16[1,27,256,256]{3,2,1,0:T(8,128)(2,1)S(1)}, bf16[1,27,256,256]{3,2,1,0:T(8,128)(2,1)}, u32[]{:S(2)}) copy-start(bf16[1,27,256,256]{3,2,1,0:T(8,128)(2,1)} %param.11) | copy-start | bytes 10616836
  18.4 19.6 %copy-start.4 = (s32[1,1,27,8,2]{2,4,3,1,0:T(2,128)S(1)}, s32[1,1,27,8,2]{2,4,3,1,0:T(2,128)}, u32[]{:S(2)}) copy-start(s32[1,1,27,8,2]{2,4,3,1,0:T(2,128)} %param.15) | copy-start | bytes 5188
  30.7 68.4 %all-to-all-start = ((bf16[27,8,2,256]{3,2,0,1:T(2,128)(2,1)}), bf16[27,8,2,256]{3,2,0,1:T(2,128)(2,1)}, u32[]{:S(2)}, u32[]{:S(2)}) async-start(bf16[27,8,2,256]{3,2,0,1:T(2,128)(2,1)} %copy.90), calls=%async_computation | async-start | bytes 442368 | tf_op jit(solution)/shard_map/all_to_all | solution.py:53
  38.0 229.4 %reduce-scatter.2.cloned.1.call-start = ((), (), s32[]{:S(2)}) async-start(), calls=%async_computation.3 | async-start | bytes 7962624 | tf_op jit(solution)/shard_map/reduce_scatter | solution.py:69
  40.0 1.4 copy-start.3
  103.1 4.7 %copy-start.5 = (pred[256]{0:T(512)(128)(4,1)S(1)}, pred[256]{0:T(512)(128)(4,1)}, u32[]{:S(2)}) copy-start(pred[256]{0:T(512)(128)(4,1)} %compare_bitcast_fusion.2) | copy-start | bytes 772
  133.1 2.3 copy-start.1
  133.1 2.3 copy-start.2
  139.4 3.6 %collective-permute-start = (bf16[256,256]{1,0:T(8,128)(2,1)}, bf16[256,256]{1,0:T(8,128)(2,1)}, u32[]{:S(2)}, u32[]{:S(2)}) collective-permute-start(bf16[256,256]{1,0:T(8,128)(2,1)} %get-tuple-element.8), channel_id=1, source_target_pairs={{8,0},{16,8},{24,16},{9,1},{17,9},{25,17},{10,2},{18,10},{26,18},{... | collective-permute-start | bytes 393224 | tf_op jit(solution)/shard_map/ppermute | solution.py:12
Sparse Core Ops, SparseCore 0:
  139.6 127.7 reduce-scatter.1
where the time goes:
time: 278 us; the launch traced here: 276 us
  waiting for transfers between devices  127 us (46%)
  local copies, waits for them, and re-layouts  71 us (26%)
  other arithmetic  29.3 us (11%)
  between operations  14.2 us (5%)
  blocking collectives  13.7 us (5%)
  matrix products  12.3 us (4%)
  starting transfers between devices  8.61 us (3%)
    reduce_scatter x1, waiting for transfers between devices, body(): lax.psum_scatter((weight_grad * loss_scale).reshape(offsets * channels, c...  124 us
    gather x6, local copies, waits for them, and re-layouts, take_rows(): picked = jnp.take(source, jnp.maximum(row_index, 0), axis=0)  34.5 us
    all_to_all x1, blocking collectives, body(): lax.all_to_all(take_rows(xmask, recv_map, nothing), 'space', split_axis=1...  13.7 us
    select_n x3, other arithmetic, take_rows(): return jnp.where((row_index >= 0)[..., None], picked, nothing)  12.3 us
    select_n x2, local copies, waits for them, and re-layouts, take_rows(): return jnp.where((row_index >= 0)[..., None], picked, nothing)  8.23 us
    all_to_all x1, starting transfers between devices, body(): lax.all_to_all(partial_value, 'space', split_axis=1, concat_axis=1, tiled...  7.28 us
  transfers between devices with their start and end apart: 3, of which 2 were waited for; matrix products, arithmetic and copies ran while one was open for 22% of the time, Pallas kernels for 0%

commit v1 on v0

--- a/solution.py
+++ b/solution.py
@@ -4,6 +4,18 @@
 from jax.sharding import PartitionSpec as P
 
 BLOCK = 128
+
+
+def in_blocks(x, dim, length):
+    lengths = x.shape
+    blocks = x.reshape(*lengths[:dim], length, lengths[dim] // length, *lengths[dim + 1 :])
+    return jnp.moveaxis(blocks, dim, 0)
+
+
+def joined_along(blocks, dim):
+    dims = list(blocks.shape[1:])
+    dims[dim] *= blocks.shape[0]
+    return jnp.moveaxis(blocks, 0, dim).reshape(dims)
 
 
 def from_behind(block, axis, distance):
@@ -51,9 +63,15 @@
         .reshape(outgoing.shape)
     )
     arrived = lax.all_to_all(partial_value, "space", split_axis=1, concat_axis=1, tiled=True)
-    returned = lax.all_to_all(
-        take_rows(xmask, recv_map, nothing), "space", split_axis=1, concat_axis=1, tiled=True
-    )
+    x = take_rows(xmask, recv_map, nothing)
+    count, mine = (lax.axis_size("space"), lax.axis_index("space"))
+    blocks = in_blocks(x, 1, count)
+    outs = [blocks[mine]]
+    for step in range(1, count):
+        sent = blocks[mine ^ step]
+        outs.append(lax.ppermute(sent, "space", [(i_2, i_2 ^ step) for i_2 in range(count)]))
+    blocks = jnp.stack(outs)[mine ^ jnp.arange(count)]
+    returned = joined_along(blocks, 1)
     weight_grad = weight_grad + lax.dot_general(
         outgoing.reshape(flat_shape),
         returned.reshape(flat_shape),

time: 278 us -> 292 us (1.050)
  blocking collectives: 13.7 us -> 0 us
  starting transfers between devices: 8.61 us -> 20.9 us
  local copies, waits for them, and re-layouts: 71 us -> 79.7 us
  other arithmetic: 29.3 us -> 32.6 us
  waiting for transfers between devices: 127 us -> 130 us
    all_to_all x1 -> x0, blocking collectives: 13.7 us -> none  [body(): lax.all_to_all(take_rows(xmask, recv_map, nothing), 'space', split_axis=1...]
    ppermute x0 -> x7, starting transfers between devices: none -> 12.3 us  [body(): lax.ppermute(sent, 'space', [(i_2, i_2 ^ step) for i_2 in range(count)])]
    unnamed x14 -> x23, local copies, waits for them, and re-layouts: 2.38 us -> 6.79 us
    ppermute x0 -> x7, waiting for transfers between devices: none -> 3.47 us  [body(): lax.ppermute(sent, 'space', [(i_2, i_2 ^ step) for i_2 in range(count)])]
    select_n x2 -> x1, local copies, waits for them, and re-layouts: 8.23 us -> 7.43 us  [take_rows(): return jnp.where((row_index >= 0)[..., None], picked, nothing)]
  transfers between devices with their start and end apart: 3 -> 10, of which waited for: 2 -> 4; matrix products, arithmetic and copies ran while one was open for 22% -> 22% of each run, Pallas kernels for 0% -> 0%
where the time goes in v1:
time: 292 us; the launch traced here: 290 us
  waiting for transfers between devices  130 us (45%)
  local copies, waits for them, and re-layouts  79.7 us (27%)
  other arithmetic  32.6 us (11%)
  starting transfers between devices  20.9 us (7%)
  between operations  14.2 us (5%)
  matrix products  12.3 us (4%)
    reduce_scatter x1, waiting for transfers between devices, body(): lax.psum_scatter((weight_grad * loss_scale).reshape(offsets * channels, c...  125 us
    gather x6, local copies, waits for them, and re-layouts, take_rows(): picked = jnp.take(source, jnp.maximum(row_index, 0), axis=0)  34.4 us
    ppermute x7, starting transfers between devices, body(): lax.ppermute(sent, 'space', [(i_2, i_2 ^ step) for i_2 in range(count)])  12.3 us
    select_n x3, other arithmetic, take_rows(): return jnp.where((row_index >= 0)[..., None], picked, nothing)  11.5 us
    select_n x1, local copies, waits for them, and re-layouts, take_rows(): return jnp.where((row_index >= 0)[..., None], picked, nothing)  7.43 us
    all_to_all x1, starting transfers between devices, body(): lax.all_to_all(partial_value, 'space', split_axis=1, concat_axis=1, tiled...  7.28 us
    unnamed x23, local copies, waits for them, and re-layouts  6.79 us
  transfers between devices with their start and end apart: 10, of which 4 were waited for; matrix products, arithmetic and copies ran while one was open for 22% of the time, Pallas kernels for 0%

profile of v1, /device:TPU:0, one launch (start us, length us, event | category | flops | bytes accessed | tf_op | source)
XLA Modules:
  0.0 289.9 jit_solution(3082822662594912353)
XLA Ops:
  7.2 1.4 compare_bitcast_fusion.1
  8.6 1.3 compare_and_fusion.1
  9.9 1.2 compare_bitcast_fusion.2
  11.2 1.3 compare_and_fusion
  12.5 1.4 copy.89
  13.9 1.4 copy.88
  15.3 0.8 copy.97
  16.1 1.0 reshape.200
  17.2 0.8 copy.90
  17.9 1.0 reshape.196
  19.0 1.7 bitcast_select_fusion.1
  20.7 3.1 %gather_fusion.2 = bf16[432,256]{1,0:T(8,128)(2,1)} fusion(bf16[256,256]{1,0:T(8,128)(2,1)} %bitcast_select_fusion.1, s32[1024]{0:T(1024)S(1)} %get-tuple-element.17), kind=kCustom, calls=%fused_computation.clone | custom fusion | bytes 444096 | tf_op jit(solution)/shard_map/jit(_take)/gather | solution.py:28
  23.8 1.7 reshape.199
  25.5 2.2 broadcast_select_fusion.3
  27.7 1.7 reshape.144
  29.4 2.2 fusion.4
  31.6 1.7 reshape.145
  33.3 1.8 copy.91
  35.1 7.3 %all-to-all-start = ((bf16[27,8,2,256]{3,2,0,1:T(2,128)(2,1)}), bf16[27,8,2,256]{3,2,0,1:T(2,128)(2,1)}, u32[]{:S(2)}, u32[]{:S(2)}) async-start(bf16[27,8,2,256]{3,2,0,1:T(2,128)(2,1)} %copy.91), calls=%async_computation | async-start | bytes 442368 | tf_op jit(solution)/shard_map/all_to_all | solution.py:65
  43.6 0.8 broadcast_maximum_fusion
  44.4 1.4 broadcast_compare_fusion
  46.4 1.5 copy.114
  47.9 0.8 copy.87
  48.7 1.3 pad_clamp_fusion.1
  50.0 0.8 copy.96
  50.7 1.4 copy.95
  52.2 1.4 copy.84
  53.6 1.5 copy.113
  55.0 1.7 reshape.166
  56.8 1.4 pad_clamp_fusion
  58.1 1.0 squeeze.37
  59.2 18.5 %gather_fusion = bf16[6912,256]{1,0:T(8,128)(2,1)} fusion(bf16[256,256]{1,0:T(8,128)(2,1)} %bitcast_select_fusion.1, s32[7168]{0:T(1024)} %pad_clamp_fusion), kind=kCustom, calls=%fused_computation.2 | custom fusion | bytes 7105536 | tf_op jit(solution)/shard_map/jit(_take)/gather | solution.py:28
  77.6 6.4 %reshape.165 = bf16[256,27,256]{2,1,0:T(8,128)(2,1)} reshape(bf16[6912,256]{1,0:T(8,128)(2,1)} %gather_fusion) | data formatting | bytes 7077888 | tf_op jit(solution)/shard_map/jit(_take)/gather | solution.py:28
  84.0 7.7 %select_select_fusion = bf16[256,27,256]{2,1,0:T(8,128)(2,1)} fusion(bf16[256,27,256]{2,1,0:T(8,128)(2,1)} %reshape.165, pred[256,27]{1,0:T(8,128)(4,1)} %copy.84, pred[256,27]{1,0:T(8,128)(4,1)} %bitcast.90), kind=kLoop, calls=%fused_computation.6 | loop fusion | flops 3538944 | bytes 7091712 | tf_op jit(solution)/shard_map/jit(_where)/select_n | solution.py:29
  91.7 7.4 %copy.94 = bf16[256,27,256]{0,2,1:T(8,128)(2,1)} copy(bf16[256,27,256]{2,1,0:T(8,128)(2,1)} %select_select_fusion) | data formatting | bytes 7077888 | tf_op jit(solution)/shard_map/jit(_where)/select_n | solution.py:29
  99.1 3.8 %fusion.7 = f32[256,256]{1,0:T(8,128)} fusion(bf16[256,27,256]{0,2,1:T(8,128)(2,1)} %copy.94, bf16[1,27,256,256]{3,2,1,0:T(8,128)(2,1)S(1)} %copy-done), kind=kOutput, calls=%fused_computation.12 | convolution fusion | flops 905969664 | bytes 7340032 | tf_op jit(solution)/shard_map/dot_general | solution.py:45
  102.9 1.0 copy_convert_fusion
  103.9 1.0 copy.93
  104.9 2.1 reshape.186
  107.0 4.7 %scatter_fusion = f32[256,256]{1,0:T(8,128)} fusion(f32[256,256]{1,0:T(8,128)} %fusion.7, s32[432]{0:T(512)S(1)} %bitcast.91, f32[432,256]{1,0:T(8,128)} %reshape.186), kind=kCustom, calls=%fused_computation.4 | custom fusion | flops 110592 | bytes 1328832 | tf_op jit(solution)/shard_map/scatter-add | solution.py:83
  111.7 1.8 bitcast_select_fusion
  113.6 3.1 %gather_fusion.3 = bf16[432,256]{1,0:T(8,128)(2,1)} fusion(bf16[256,256]{1,0:T(8,128)(2,1)} %get-tuple-element.14, s32[1024]{0:T(1024)S(1)} %get-tuple-element.16), kind=kCustom, calls=%fused_computation.1.clone | custom fusion | bytes 444096 | tf_op jit(solution)/shard_map/jit(_take)/gather | solution.py:28
  116.7 1.7 reshape.203
  118.4 1.6 broadcast_select_fusion.2
  120.1 2.0 collective-permute-start.1
  122.8 3.3 %collective-permute-start.7 = (bf16[27,1,2,256]{3,2,1,0:T(2,128)(2,1)S(1)}, bf16[27,1,2,256]{3,2,1,0:T(2,128)(2,1)S(1)}, u32[]{:S(2)}, u32[]{:S(2)}) collective-permute-start(bf16[27,1,2,256]{3,2,1,0:T(2,128)(2,1)S(1)} %get-tuple-element.7), channel_id=1, source_target_pairs={{0,7},{1,6},{2,5},{3,4},{4,3},{5,2},{6,1},{7,0},{8,15},{9,14},{10,... | collective-permute-start | bytes 82952 | tf_op jit(solution)/shard_map/ppermute | solution.py:72
  126.6 3.3 %collective-permute-start.4 = (bf16[27,1,2,256]{3,2,0,1:T(2,128)(2,1)S(1)}, bf16[27,1,2,256]{3,2,0,1:T(2,128)(2,1)S(1)}, u32[]{:S(2)}, u32[]{:S(2)}) collective-permute-start(bf16[27,1,2,256]{3,2,0,1:T(2,128)(2,1)S(1)} %get-tuple-element.9), channel_id=1, source_target_pairs={{0,4},{1,5},{2,6},{3,7},{4,0},{5,1},{6,2},{7,3},{8,12},{9,13},{10,... | collective-permute-start | bytes 82952 | tf_op jit(solution)/shard_map/ppermute | solution.py:72
  129.9 2.0 collective-permute-start.2
  132.5 1.5 collective-permute-done.2
  134.0 1.2 collective-permute-start.6
  135.8 0.6 bitcast_dynamic-update-slice_fusion.4
  136.4 0.6 bitcast_dynamic-update-slice_fusion.3
  137.1 0.6 bitcast_dynamic-update-slice_fusion.2
  137.7 2.0 collective-permute-done.6
  140.3 0.6 bitcast_dynamic-update-slice_fusion
  140.9 2.7 gather_fusion.1
  143.6 1.8 copy.104
  145.4 1.7 reshape_reshape.3
  147.1 2.3 fusion.12
  149.4 4.0 %add_multiply_fusion = f32[27,256,256]{2,1,0:T(8,128)} fusion(f32[27,256,256]{2,1,0:T(8,128)S(1)} %fusion.12, bf16[256,27,256]{0,2,1:T(8,128)(2,1)S(1)} %copy-done.1, bf16[256,256]{1,0:T(8,128)(2,1)S(1)} %copy-done.2), kind=kOutput, calls=%fused_computation.5 | convolution fusion | flops 909508608 | bytes 17825792 | tf_op jit(solution)/shard_map/dot_general | solution.py:48
  153.4 1.3 collective-permute-start
  154.7 2.3 collective-permute-done
  157.0 124.5 %reduce-scatter.2.cloned.1.call-done = f32[864,256]{1,0:T(8,128)} async-done(((f32[6912,256]{1,0:T(8,128)}), f32[864,256]{1,0:T(8,128)}) %reduce-scatter.2.cloned.1.call-update) | async-done | bytes 884752 | tf_op jit(solution)/shard_map/reduce_scatter | solution.py:87
  281.5 1.6 copy.126
  (34 shorter events, 5.1 us)
Async XLA Ops:
  7.2 22.3 %copy-start = (bf16[1,27,256,256]{3,2,1,0:T(8,128)(2,1)S(1)}, bf16[1,27,256,256]{3,2,1,0:T(8,128)(2,1)}, u32[]{:S(2)}) copy-start(bf16[1,27,256,256]{3,2,1,0:T(8,128)(2,1)} %param.11) | copy-start | bytes 10616836
  23.8 19.3 %copy-start.4 = (s32[1,1,27,8,2]{2,4,3,1,0:T(2,128)S(1)}, s32[1,1,27,8,2]{2,4,3,1,0:T(2,128)}, u32[]{:S(2)}) copy-start(s32[1,1,27,8,2]{2,4,3,1,0:T(2,128)} %param.15) | copy-start | bytes 5188
  23.8 26.2 %copy-start.5 = (pred[27,8,2]{0,2,1:T(4,128)(4,1)S(1)}, pred[27,8,2]{0,2,1:T(4,128)(4,1)}, u32[]{:S(2)}) copy-start(pred[27,8,2]{0,2,1:T(4,128)(4,1)} %get-tuple-element.3) | copy-start | bytes 1300
  35.1 67.8 %all-to-all-start = ((bf16[27,8,2,256]{3,2,0,1:T(2,128)(2,1)}), bf16[27,8,2,256]{3,2,0,1:T(2,128)(2,1)}, u32[]{:S(2)}, u32[]{:S(2)}) async-start(bf16[27,8,2,256]{3,2,0,1:T(2,128)(2,1)} %copy.91), calls=%async_computation | async-start | bytes 442368 | tf_op jit(solution)/shard_map/all_to_all | solution.py:65
  42.4 239.1 %reduce-scatter.2.cloned.1.call-start = ((), (), s32[]{:S(2)}) async-start(), calls=%async_computation.2 | async-start | bytes 7962624 | tf_op jit(solution)/shard_map/reduce_scatter | solution.py:87
  44.4 1.4 copy-start.3
  107.0 4.7 %copy-start.6 = (pred[256]{0:T(512)(128)(4,1)S(1)}, pred[256]{0:T(512)(128)(4,1)}, u32[]{:S(2)}) copy-start(pred[256]{0:T(512)(128)(4,1)} %compare_bitcast_fusion.2) | copy-start | bytes 772
  120.1 9.7 %collective-permute-start.1 = (bf16[27,1,2,256]{3,2,0,1:T(2,128)(2,1)S(1)}, bf16[27,1,2,256]{3,2,0,1:T(2,128)(2,1)S(1)}, u32[]{:S(2)}, u32[]{:S(2)}) collective-permute-start(bf16[27,1,2,256]{3,2,0,1:T(2,128)(2,1)S(1)} %get-tuple-element.12), channel_id=1, source_target_pairs={{0,1},{1,0},{2,3},{3,2},{4,5},{5,4},{6,7},{7,6},{8,9},{9,8},{10,11... | collective-permute-start | bytes 82952 | tf_op jit(solution)/shard_map/ppermute | solution.py:72
  122.8 17.5 %collective-permute-start.7 = (bf16[27,1,2,256]{3,2,1,0:T(2,128)(2,1)S(1)}, bf16[27,1,2,256]{3,2,1,0:T(2,128)(2,1)S(1)}, u32[]{:S(2)}, u32[]{:S(2)}) collective-permute-start(bf16[27,1,2,256]{3,2,1,0:T(2,128)(2,1)S(1)} %get-tuple-element.7), channel_id=1, source_target_pairs={{0,7},{1,6},{2,5},{3,4},{4,3},{5,2},{6,1},{7,0},{8,15},{9,14},{10,... | collective-permute-start | bytes 82952 | tf_op jit(solution)/shard_map/ppermute | solution.py:72
  126.0 11.1 %collective-permute-start.5 = (bf16[27,1,2,256]{3,2,0,1:T(2,128)(2,1)S(1)}, bf16[27,1,2,256]{3,2,0,1:T(2,128)(2,1)S(1)}, u32[]{:S(2)}, u32[]{:S(2)}) collective-permute-start(bf16[27,1,2,256]{3,2,0,1:T(2,128)(2,1)S(1)} %get-tuple-element.8), channel_id=1, source_target_pairs={{0,5},{1,4},{2,7},{3,6},{4,1},{5,0},{6,3},{7,2},{8,13},{9,12},{10,... | collective-permute-start | bytes 82952 | tf_op jit(solution)/shard_map/ppermute | solution.py:72
  126.6 9.9 %collective-permute-start.4 = (bf16[27,1,2,256]{3,2,0,1:T(2,128)(2,1)S(1)}, bf16[27,1,2,256]{3,2,0,1:T(2,128)(2,1)S(1)}, u32[]{:S(2)}, u32[]{:S(2)}) collective-permute-start(bf16[27,1,2,256]{3,2,0,1:T(2,128)(2,1)S(1)} %get-tuple-element.9), channel_id=1, source_target_pairs={{0,4},{1,5},{2,6},{3,7},{4,0},{5,1},{6,2},{7,3},{8,12},{9,13},{10,... | collective-permute-start | bytes 82952 | tf_op jit(solution)/shard_map/ppermute | solution.py:72
  129.8 6.0 %collective-permute-start.3 = (bf16[27,1,2,256]{3,2,0,1:T(2,128)(2,1)S(1)}, bf16[27,1,2,256]{3,2,0,1:T(2,128)(2,1)S(1)}, u32[]{:S(2)}, u32[]{:S(2)}) collective-permute-start(bf16[27,1,2,256]{3,2,0,1:T(2,128)(2,1)S(1)} %get-tuple-element.10), channel_id=1, source_target_pairs={{0,3},{1,2},{2,1},{3,0},{4,7},{5,6},{6,5},{7,4},{8,11},{9,10},{10,... | collective-permute-start | bytes 82952 | tf_op jit(solution)/shard_map/ppermute | solution.py:72
  129.9 4.2 %collective-permute-start.2 = (bf16[27,1,2,256]{3,2,0,1:T(2,128)(2,1)S(1)}, bf16[27,1,2,256]{3,2,0,1:T(2,128)(2,1)S(1)}, u32[]{:S(2)}, u32[]{:S(2)}) collective-permute-start(bf16[27,1,2,256]{3,2,0,1:T(2,128)(2,1)S(1)} %get-tuple-element.11), channel_id=1, source_target_pairs={{0,2},{1,3},{2,0},{3,1},{4,6},{5,7},{6,4},{7,5},{8,10},{9,11},{10,... | collective-permute-start | bytes 82952 | tf_op jit(solution)/shard_map/ppermute | solution.py:72
  134.0 5.7 %collective-permute-start.6 = (bf16[27,1,2,256]{3,2,0,1:T(2,128)(2,1)S(1)}, bf16[27,1,2,256]{3,2,0,1:T(2,128)(2,1)S(1)}, u32[]{:S(2)}, u32[]{:S(2)}) collective-permute-start(bf16[27,1,2,256]{3,2,0,1:T(2,128)(2,1)S(1)} %get-tuple-element.13), channel_id=1, source_target_pairs={{0,6},{1,7},{2,4},{3,5},{4,2},{5,3},{6,0},{7,1},{8,14},{9,15},{10,... | collective-permute-start | bytes 82952 | tf_op jit(solution)/shard_map/ppermute | solution.py:72
  147.1 2.3 copy-start.1
  147.1 2.3 copy-start.2
  153.4 3.6 %collective-permute-start = (bf16[256,256]{1,0:T(8,128)(2,1)}, bf16[256,256]{1,0:T(8,128)(2,1)}, u32[]{:S(2)}, u32[]{:S(2)}) collective-permute-start(bf16[256,256]{1,0:T(8,128)(2,1)} %get-tuple-element.15), channel_id=1, source_target_pairs={{8,0},{16,8},{24,16},{9,1},{17,9},{25,17},{10,2},{18,10},{26,18},{... | collective-permute-start | bytes 393224 | tf_op jit(solution)/shard_map/ppermute | solution.py:24
Sparse Core Ops, SparseCore 0:
  153.5 127.9 reduce-scatter.1
